TPU v7x, 128 devices: a whole 4x4x4 slice. The times are simulated.
128 devices in a mesh: pr: 16 (over z, x), pc: 8 (over y, core).
Axes of the slice: x: 4, y: 4, z: 4, core: 2. Of those that a mesh axis runs over, the one named last changes fastest.
Arguments:
- trailing: float32 [20480, 20480], P('pr', 'pc'), may hold values from -25 to 25, as said below
- v_panels: float32 [6, 32, 20480], P(None, None, ('pr', 'pc')), may hold values from -0.078125 to 0.078125
- t_panels: float32 [6, 32, 32], replicated, may hold values from -0.2 to 0.5, as said below
Outputs:
- updated: float32 [20480, 20480], P('pr', 'pc')
- w_panels: float32 [6, 32, 20480], P(None, None, ('pr', 'pc'))
Inputs may be any that keep to these rules, and one draw needn't show every extreme that they name: trailing is exactly symmetric. `t_panels`: each panel's factor is upper triangular with diagonal entries of 0.25 to 0.5.
All inputs are finite; a program needn't handle non-finite values.
Results may differ from a plain program's by a relative error of at most 0.00013.
Values sent between devices are 32-bit elements; how exact they have to be, the bound alone decides.
A program may use at most 128 MiB of HBM per device.

v0:
```python
import jax
import jax.numpy as jnp
from jax import lax
from jax.sharding import PartitionSpec as P

HIGHEST = lax.Precision.HIGHEST


def contract(left_side, right_side, left_dim, right_dim, precision=HIGHEST):
    return lax.dot_general(
        left_side,
        right_side,
        (((left_dim,), (right_dim,)), ((), ())),
        precision=precision,
        preferred_element_type=jnp.float32,
    )


def small_coefficients(gram_y, gram_v, t_panels):
    panels, width, _ = t_panels.shape
    size = panels * width
    eye = jnp.eye(size, dtype=jnp.float32)
    zero = jnp.zeros((size, size), jnp.float32)
    of_y = jnp.concatenate([gram_y, zero, eye], axis=1)
    of_v = jnp.concatenate([gram_v, eye, zero], axis=1)
    of_w = []
    for panel in range(panels):
        here = slice(panel * width, (panel + 1) * width)
        of_x = of_y[here]
        if panel:
            done = jnp.concatenate(of_w, axis=0)
            before = slice(0, panel * width)
            left = jnp.concatenate([done[:, here], gram_v[before, here]], axis=0)
            right = jnp.concatenate([of_v[before], done], axis=0)
            of_x = of_x - contract(left, right, 0, 0)
        factor = t_panels[panel]
        scaled = contract(factor, of_x, 0, 0)
        middle = contract(scaled[:, here], factor, 1, 0)
        of_w.append(scaled - 0.5 * contract(middle, of_v[here], 1, 0))
    return jnp.concatenate(of_w, axis=0)


def per_device(trailing, v_panels, t_panels):
    rows, cols = (lax.axis_size("pr"), lax.axis_size("pc"))
    ratio = rows // cols
    panels, width, share = v_panels.shape
    size = panels * width
    v_own = v_panels.reshape(size, share)
    moves = []
    for i in range(rows):
        for j in range(cols):
            moves.append((i * cols + j, (i % ratio * cols + j) * cols + i // ratio))

    def columns(own):
        return lax.all_gather(lax.ppermute(own, ("pr", "pc"), moves), "pr", axis=1, tiled=True)

    v_row = lax.all_gather(v_own, "pc", axis=1, tiled=True)
    v_col = columns(v_own)
    partial_y = contract(v_col, trailing, 1, 1, lax.Precision.HIGH)
    y_own = lax.psum_scatter(partial_y, "pc", scatter_dimension=1, tiled=True)
    y_row = lax.all_gather(y_own, "pc", axis=1, tiled=True)
    y_col = columns(y_own)
    grams = contract(v_own, jnp.concatenate([y_own, v_own], axis=0), 1, 1)
    grams = lax.psum(grams, ("pr", "pc"))
    coefs = small_coefficients(grams[:, :size], grams[:, size:], t_panels)
    of_v, of_y = (coefs[:, size : 2 * size], coefs[:, 2 * size :])
    w_own = contract(of_v, v_own, 1, 0) + contract(of_y, y_own, 1, 0)
    left_v = contract(of_v + of_v.T, v_row, 1, 0) + contract(of_y, y_row, 1, 0)
    left_y = contract(of_y, v_row, 0, 0)
    left = jnp.concatenate([left_v, left_y], axis=0)
    right = jnp.concatenate([v_col, y_col], axis=0)
    matrix = trailing - contract(left, right, 0, 0, lax.Precision.HIGH)
    return (matrix, w_own.reshape(panels, width, share))


def solution(mesh):
    return jax.shard_map(
        per_device,
        mesh=mesh,
        in_specs=(P("pr", "pc"), P(None, None, ("pr", "pc")), P()),
        out_specs=(P("pr", "pc"), P(None, None, ("pr", "pc"))),
        check_vma=False,
    )
```

profile of v0, /device:TPU:1, one launch (start us, length us, event | category | flops | bytes accessed | tf_op | source)
XLA Modules:
  0.0 353.8 jit_solution(15385846826090534265)
XLA Ops:
  7.2 1.0 copy.12
  8.2 4.5 %collective-permute-start = (f32[192,160]{0,1:T(8,128)S(1)}, f32[192,160]{0,1:T(8,128)S(1)}, u32[]{:S(2)}, u32[]{:S(2)}) collective-permute-start(f32[192,160]{0,1:T(8,128)S(1)} %copy.12), channel_id=1, source_target_pairs={{0,0},{1,8},{2,16},{3,24},{4,32},{5,40},{6,48},{7,56},{8,64},{9,72... | collective-permute-start | bytes 368648 | tf_op jit(solution)/shard_map/ppermute | solution.py:55
  12.8 4.5 %collective-permute-done = f32[192,160]{0,1:T(8,128)S(1)} collective-permute-done((f32[192,160]{0,1:T(8,128)S(1)}, f32[192,160]{0,1:T(8,128)S(1)}, u32[]{:S(2)}, u32[]{:S(2)}) %collective-permute-start) | collective-permute-done | bytes 122912 | tf_op jit(solution)/shard_map/ppermute | solution.py:55
  18.0 53.5 %all-gather.3.cloned.1.call-done = f32[192,2560]{0,1:T(8,128)} async-done(((f32[192,160]{0,1:T(8,128)}), f32[192,2560]{0,1:T(8,128)}) %all-gather.3.cloned.1.call-update) | async-done | bytes 1966096 | tf_op jit(solution)/shard_map/all_gather | solution.py:55
  71.5 9.9 %fusion.106 = f32[192,1280]{0,1:T(8,128)} fusion(f32[192,2560]{0,1:T(8,128)} %all-gather.3.cloned.1.call-done, f32[1280,2560]{1,0:T(8,128)} %param.3), kind=kOutput, calls=%fused_computation.158 | convolution fusion | flops 3774873600 | bytes 16056320 | tf_op jit(solution)/shard_map/dot_general | solution.py:10
  81.5 0.7 fusion.29
  82.2 15.8 %all_gather.13 = f32[192,1280]{0,1:T(8,128)S(1)} all-gather(f32[192,160]{0,1:T(8,128)S(1)} %copy.12), channel_id=1, replica_groups=mesh['pr'=16,'pc'=8] {'pc'}, dimensions={1}, use_global_device_ids=true | all-gather | bytes 1105920 | tf_op jit(solution)/shard_map/all_gather | solution.py:57
  98.0 13.6 %reduce-scatter.2.cloned.1.call-done = f32[192,160]{0,1:T(8,128)} async-done(((f32[192,1280]{0,1:T(8,128)}), f32[192,160]{0,1:T(8,128)}) %reduce-scatter.2.cloned.1.call-update) | async-done | bytes 122896 | tf_op jit(solution)/shard_map/reduce_scatter | solution.py:60
  111.6 2.2 convolution_bitcast_fusion
  113.9 6.3 %collective-permute-start.1 = (f32[192,160]{0,1:T(8,128)}, f32[192,160]{0,1:T(8,128)S(1)}, u32[]{:S(2)}, u32[]{:S(2)}) collective-permute-start(f32[192,160]{0,1:T(8,128)} %reduce-scatter.2.cloned.1.call-done), channel_id=1, source_target_pairs={{0,0},{1,8},{2,16},{3,24},{4,32},{5,40},{6,48},{7,56},{8,64},{9,72... | collective-permute-start | bytes 368648 | tf_op jit(solution)/shard_map/ppermute | solution.py:55
  120.2 20.7 %all_gather.14 = f32[192,1280]{0,1:T(8,128)S(1)} all-gather(f32[192,160]{0,1:T(8,128)} %reduce-scatter.2.cloned.1.call-done), channel_id=1, replica_groups=mesh['pr'=16,'pc'=8] {'pc'}, dimensions={1}, use_global_device_ids=true | all-gather | bytes 1105920 | tf_op jit(solution)/shard_map/all_gather | solution.py:61
  140.9 0.7 copy-done.4
  141.6 118.4 %all-reduce.2.cloned.1.call-done = f32[192,384]{1,0:T(8,128)} async-done(((f32[192,384]{1,0:T(8,128)}), f32[192,384]{1,0:T(8,128)}) %all-reduce.2.cloned.1.call-update) | async-done | bytes 294928 | tf_op jit(solution)/shard_map/psum | solution.py:64
  260.0 1.1 fusion.105
  261.2 2.0 pad_maximum_fusion.1
  263.2 0.7 slice.186
  263.9 0.7 slice.191
  264.6 0.8 slice_dynamic-update-slice_fusion.1
  265.4 0.8 slice_dynamic-update-slice_fusion
  266.1 0.8 slice.185
  267.6 0.9 slice.190
  268.5 0.7 copy.17
  269.1 1.2 convolution_bitcast_fusion.6
  270.3 0.9 fusion.66
  271.2 0.9 constant_dynamic-update-slice_fusion.8
  272.2 0.8 slice.181
  272.9 1.2 convolution_subtract_fusion.3
  274.1 1.0 convolution_bitcast_fusion.5
  275.1 0.9 fusion.64
  276.0 0.9 constant_dynamic-update-slice_fusion.7
  277.0 0.8 copy-done.6
  277.9 1.3 convolution_subtract_fusion.5
  279.2 1.0 convolution_bitcast_fusion.4
  280.2 0.9 fusion.62
  281.1 1.0 constant_dynamic-update-slice_fusion.6
  282.1 0.7 pad_maximum_fusion.5
  282.8 1.5 copy.16
  284.2 1.5 convolution_subtract_fusion.4
  285.8 1.0 convolution_bitcast_fusion.3
  287.4 1.5 fusion.60
  288.9 1.5 slice.195
  290.5 1.5 copy.19
  292.0 1.6 slice.201
  293.6 1.6 copy.21
  295.2 1.9 constant_dynamic-update-slice_fusion.5
  297.7 0.9 copy.18
  298.6 1.6 convolution_subtract_fusion.2
  300.2 1.0 convolution_bitcast_fusion.2
  301.2 0.9 fusion.58
  302.0 0.9 constant_dynamic-update-slice_fusion.4
  303.0 1.0 slice.200
  303.9 0.7 copy.20
  304.6 1.8 convolution_subtract_fusion.1
  306.4 1.0 convolution_bitcast_fusion.1
  307.4 0.9 fusion.56
  308.3 0.9 fusion.7
  309.2 1.1 slice.205
  310.3 1.3 fusion.30
  311.5 1.6 convolution_add_fusion.1
  313.1 0.8 copy.24
  314.0 3.9 %fusion.32 = f32[192,1280]{1,0:T(8,128)} fusion(f32[192,1280]{0,1:T(8,128)S(1)} %all_gather.13, f32[192,576]{1,0:T(8,128)} %fusion.7), kind=kOutput, calls=%fused_computation.59 | convolution fusion | flops 566231040 | bytes 2162688 | tf_op jit(solution)/shard_map/dot_general | solution.py:10
  317.9 2.4 fusion.28
  320.4 3.4 convolution_add_fusion
  323.8 23.5 %convolution_subtract_fusion = f32[1280,2560]{1,0:T(8,128)} fusion(f32[1280,2560]{1,0:T(8,128)} %param.3, f32[192,2560]{0,1:T(8,128)} %all-gather.5.cloned.1.call-done, f32[192,2560]{0,1:T(8,128)} %all-gather.3.cloned.1.call-done, f32[192,1280]{1,0:T(8,128)S(1)} %copy-done, f32[192,1280]{1,0:T(8,128)} %convolution_add_fusion), kind=kOutput, calls=%fused_computation | convolution fusion | flops 7554498560 | bytes 32112640 | tf_op jit(solution)/shard_map/dot_general | solution.py:10
  (30 shorter events, 3.2 us)
Async XLA Ops:
  7.2 64.3 %all-gather.3.cloned.1.call-start = ((), (), s32[]{:S(2)}) async-start(), calls=%async_computation.1 | async-start | bytes 2785280 | tf_op jit(solution)/shard_map/all_gather | solution.py:55
  8.2 9.0 %collective-permute-start = (f32[192,160]{0,1:T(8,128)S(1)}, f32[192,160]{0,1:T(8,128)S(1)}, u32[]{:S(2)}, u32[]{:S(2)}) collective-permute-start(f32[192,160]{0,1:T(8,128)S(1)} %copy.12), channel_id=1, source_target_pairs={{0,0},{1,8},{2,16},{3,24},{4,32},{5,40},{6,48},{7,56},{8,64},{9,72... | collective-permute-start | bytes 368648 | tf_op jit(solution)/shard_map/ppermute | solution.py:55
  17.3 0.7 copy-start.5
  18.0 93.6 %reduce-scatter.2.cloned.1.call-start = ((), (), s32[]{:S(2)}) async-start(), calls=%async_computation.2 | async-start | bytes 1474560 | tf_op jit(solution)/shard_map/reduce_scatter | solution.py:60
  81.4 30.2 %copy-start.1 = (f32[6,32,160]{2,1,0:T(8,128)S(1)}, f32[6,32,160]{2,1,0:T(8,128)}, u32[]{:S(2)}) copy-start(f32[6,32,160]{2,1,0:T(8,128)} %param.4) | copy-start | bytes 368644
  81.5 178.6 %all-reduce.2.cloned.1.call-start = ((), (), s32[]{:S(2)}) async-start(), calls=%async_computation.3 | async-start | bytes 589824 | tf_op jit(solution)/shard_map/psum | solution.py:64
  113.8 210.0 %all-gather.5.cloned.1.call-start = ((), (), s32[]{:S(2)}) async-start(), calls=%async_computation.4 | async-start | bytes 2785280 | tf_op jit(solution)/shard_map/all_gather | solution.py:55
  113.9 27.0 %collective-permute-start.1 = (f32[192,160]{0,1:T(8,128)}, f32[192,160]{0,1:T(8,128)S(1)}, u32[]{:S(2)}, u32[]{:S(2)}) collective-permute-start(f32[192,160]{0,1:T(8,128)} %reduce-scatter.2.cloned.1.call-done), channel_id=1, source_target_pairs={{0,0},{1,8},{2,16},{3,24},{4,32},{5,40},{6,48},{7,56},{8,64},{9,72... | collective-permute-start | bytes 368648 | tf_op jit(solution)/shard_map/ppermute | solution.py:55
  140.9 0.7 copy-start.4
  277.0 0.8 copy-start.6
  286.8 0.6 copy-start.3
  297.7 12.6 %copy-start.2 = (f32[192,160]{0,1:T(8,128)S(1)}, f32[192,160]{0,1:T(8,128)}, u32[]{:S(2)}) copy-start(f32[192,160]{0,1:T(8,128)} %reduce-scatter.2.cloned.1.call-done) | copy-start | bytes 368644
  320.3 3.4 copy-start
Sparse Core Ops, SparseCore 0:
  18.1 53.3 all-gather.2
  81.6 29.9 reduce-scatter.1
  116.9 143.0 all-reduce.1
  262.0 44.4 all-gather.4
where the time goes:
time: 355 us; the launch traced here: 354 us
  waiting for transfers between devices  190 us (54%)
  matrix products  74.1 us (21%)
  blocking collectives  36.6 us (10%)
  local copies, waits for them, and re-layouts  24.1 us (7%)
  between operations  14 us (4%)
  starting transfers between devices  11 us (3%)
  other arithmetic  4.12 us (1%)
    psum x1, waiting for transfers between devices, per_device(): grams = lax.psum(grams, ('pr', 'pc'))  118 us
    dot_general x31, matrix products, contract(): lax.dot_general(left_side, right_side, (((left_dim,), (right_dim,)), ((),...  74.1 us
    all_gather x2, waiting for transfers between devices, columns(): lax.all_gather(lax.ppermute(own, ('pr', 'pc'), moves), 'pr', axis=1, tile...  53.5 us
    all_gather x1, blocking collectives, per_device(): y_row = lax.all_gather(y_own, 'pc', axis=1, tiled=True)  20.7 us
    all_gather x1, blocking collectives, per_device(): v_row = lax.all_gather(v_own, 'pc', axis=1, tiled=True)  15.8 us
    slice x15, local copies, waits for them, and re-layouts, small_coefficients(): left = jnp.concatenate([done[:, here], gram_v[before, here]], axis=0)  14.3 us
    reduce_scatter x1, waiting for transfers between devices, per_device(): y_own = lax.psum_scatter(partial_y, 'pc', scatter_dimension=1, tiled=True)  13.6 us
    ppermute x2, starting transfers between devices, columns(): lax.ppermute(own, ('pr', 'pc'), moves)  10.8 us
  transfers between devices with their start and end apart: 6, of which 4 were waited for; matrix products, arithmetic and copies ran while one was open for 18% of the time, Pallas kernels for 0%

commit v1 on v0

--- a/solution.py
+++ b/solution.py
@@ -4,6 +4,22 @@
 from jax.sharding import PartitionSpec as P
 
 HIGHEST = lax.Precision.HIGHEST
+
+
+def gather_around(x, axis, dim):
+    ways, here, lap = (lax.axis_size(axis), lax.axis_index(axis), x.shape[dim])
+    dims = [n * ways if d == dim else n for d, n in enumerate(x.shape)]
+    full = lax.dynamic_update_slice_in_dim(jnp.zeros(dims, x.dtype), x, here * lap, axis=dim)
+    going_up = going_down = x
+    for far in range(1, ways // 2 + 1):
+        going_up = lax.ppermute(going_up, axis, [(d, (d + 1) % ways) for d in range(ways)])
+        full = lax.dynamic_update_slice_in_dim(full, going_up, (here - far) % ways * lap, axis=dim)
+        if 2 * far < ways:
+            going_down = lax.ppermute(going_down, axis, [(d, (d - 1) % ways) for d in range(ways)])
+            full = lax.dynamic_update_slice_in_dim(
+                full, going_down, (here + far) % ways * lap, axis=dim
+            )
+    return full
 
 
 def contract(left_side, right_side, left_dim, right_dim, precision=HIGHEST):
@@ -54,7 +70,7 @@
     def columns(own):
         return lax.all_gather(lax.ppermute(own, ("pr", "pc"), moves), "pr", axis=1, tiled=True)
 
-    v_row = lax.all_gather(v_own, "pc", axis=1, tiled=True)
+    v_row = gather_around(v_own, "pc", 1)
     v_col = columns(v_own)
     partial_y = contract(v_col, trailing, 1, 1, lax.Precision.HIGH)
     y_own = lax.psum_scatter(partial_y, "pc", scatter_dimension=1, tiled=True)

time: 355 us -> 338 us (0.952)
  blocking collectives: 36.6 us -> 22 us
  matrix products: 74.1 us -> 59.5 us
  starting transfers between devices: 11 us -> 21.3 us
  waiting for transfers between devices: 190 us -> 197 us
  other arithmetic: 4.12 us -> 0.39 us
    all_gather x1 -> x0, blocking collectives: 15.8 us -> none  [per_device(): v_row = lax.all_gather(v_own, 'pc', axis=1, tiled=True)]
    dot_general x31, matrix products: 74.1 us -> 59.5 us  [contract(): lax.dot_general(left_side, right_side, (((left_dim,), (right_dim,)), ((),...]
    all_gather x2, waiting for transfers between devices: 53.5 us -> 67.6 us  [columns(): lax.all_gather(lax.ppermute(own, ('pr', 'pc'), moves), 'pr', axis=1, tile...]
    reduce_scatter x1, waiting for transfers between devices: 13.6 us -> 0.02 us  [per_device(): y_own = lax.psum_scatter(partial_y, 'pc', scatter_dimension=1, tiled=True)]
    dynamic_update_slice x0 -> x8, local copies, waits for them, and re-layouts: none -> 13 us  [the longest x4 6.01 us: gather_around(): lax.dynamic_update_slice_in_dim(full, going_up, (here - far) % ways * lap...]
    slice x15, local copies, waits for them, and re-layouts: 14.3 us -> 1.89 us  [small_coefficients(): left = jnp.concatenate([done[:, here], gram_v[before, here]], axis=0)]
    ppermute x0 -> x7, starting transfers between devices: none -> 10.5 us  [the longest x4 9.52 us: gather_around(): lax.ppermute(going_up, axis, [(d, (d + 1) % ways) for d in range(ways)])]
    ppermute x0 -> x7, waiting for transfers between devices: none -> 8.65 us  [the longest x4 7.63 us: gather_around(): lax.ppermute(going_up, axis, [(d, (d + 1) % ways) for d in range(ways)])]
  transfers between devices with their start and end apart: 6 -> 13, of which waited for: 4 -> 8; matrix products, arithmetic and copies ran while one was open for 18% -> 13% of each run, Pallas kernels for 0% -> 0%
where the time goes in v1:
time: 338 us; the launch traced here: 337 us
  waiting for transfers between devices  197 us (58%)
  matrix products  59.5 us (18%)
  local copies, waits for them, and re-layouts  23.2 us (7%)
  blocking collectives  22 us (7%)
  starting transfers between devices  21.3 us (6%)
  between operations  14.1 us (4%)
    psum x1, waiting for transfers between devices, per_device(): grams = lax.psum(grams, ('pr', 'pc'))  116 us
    all_gather x2, waiting for transfers between devices, columns(): lax.all_gather(lax.ppermute(own, ('pr', 'pc'), moves), 'pr', axis=1, tile...  67.6 us
    dot_general x31, matrix products, contract(): lax.dot_general(left_side, right_side, (((left_dim,), (right_dim,)), ((),...  59.5 us
    all_gather x1, blocking collectives, per_device(): y_row = lax.all_gather(y_own, 'pc', axis=1, tiled=True)  22 us
    ppermute x2, starting transfers between devices, columns(): lax.ppermute(own, ('pr', 'pc'), moves)  10.6 us
    ppermute x4, starting transfers between devices, gather_around(): lax.ppermute(going_up, axis, [(d, (d + 1) % ways) for d in range(ways)])  9.52 us
    ppermute x4, waiting for transfers between devices, gather_around(): lax.ppermute(going_up, axis, [(d, (d + 1) % ways) for d in range(ways)])  7.63 us
  transfers between devices with their start and end apart: 13, of which 8 were waited for; matrix products, arithmetic and copies ran while one was open for 13% of the time, Pallas kernels for 0%

profile of v1, /device:TPU:1, one launch (start us, length us, event | category | flops | bytes accessed | tf_op | source)
XLA Modules:
  0.0 337.3 jit_solution(7235087431585711557)
XLA Ops:
  7.2 1.0 copy.12
  8.2 4.5 %collective-permute-start = (f32[192,160]{0,1:T(8,128)S(1)}, f32[192,160]{0,1:T(8,128)S(1)}, u32[]{:S(2)}, u32[]{:S(2)}) collective-permute-start(f32[192,160]{0,1:T(8,128)S(1)} %copy.12), channel_id=1, source_target_pairs={{0,0},{1,8},{2,16},{3,24},{4,32},{5,40},{6,48},{7,56},{8,64},{9,72... | collective-permute-start | bytes 368648 | tf_op jit(solution)/shard_map/ppermute | solution.py:71
  12.8 4.5 %collective-permute-done = f32[192,160]{0,1:T(8,128)S(1)} collective-permute-done((f32[192,160]{0,1:T(8,128)S(1)}, f32[192,160]{0,1:T(8,128)S(1)}, u32[]{:S(2)}, u32[]{:S(2)}) %collective-permute-start) | collective-permute-done | bytes 122912 | tf_op jit(solution)/shard_map/ppermute | solution.py:71
  17.3 0.7 copy-done.9
  18.0 53.5 %all-gather.3.cloned.1.call-done = f32[192,2560]{0,1:T(8,128)} async-done(((f32[192,160]{0,1:T(8,128)}), f32[192,2560]{0,1:T(8,128)}) %all-gather.3.cloned.1.call-update) | async-done | bytes 1966096 | tf_op jit(solution)/shard_map/all_gather | solution.py:71
  71.5 9.9 %fusion.106 = f32[192,1280]{0,1:T(8,128)} fusion(f32[192,2560]{0,1:T(8,128)} %all-gather.3.cloned.1.call-done, f32[1280,2560]{1,0:T(8,128)} %param.3), kind=kOutput, calls=%fused_computation.158 | convolution fusion | flops 3774873600 | bytes 16056320 | tf_op jit(solution)/shard_map/dot_general | solution.py:26
  81.5 2.1 collective-permute-start.1
  83.6 2.6 collective-permute-done.1
  86.2 2.5 collective-permute-start.3
  88.8 3.4 collective-permute-done.3
  92.2 2.5 collective-permute-start.5
  94.7 1.0 collective-permute-done.4
  95.7 0.8 collective-permute-start.6
  96.5 1.7 collective-permute-done.5
  98.2 2.5 collective-permute-start.7
  100.7 1.8 dynamic_update_slice.24
  102.6 1.5 dynamic_update_slice.25
  104.1 1.8 dynamic_update_slice.26
  105.9 1.2 dynamic_update_slice.27
  107.1 1.8 dynamic_update_slice.28
  108.9 1.5 dynamic_update_slice.29
  110.4 1.5 dynamic_update_slice.30
  112.0 1.8 dynamic_update_slice.31
  113.8 2.4 convolution_bitcast_fusion
  116.3 6.1 %collective-permute-start.8 = (f32[192,160]{0,1:T(8,128)}, f32[192,160]{0,1:T(8,128)S(1)}, u32[]{:S(2)}, u32[]{:S(2)}) collective-permute-start(f32[192,160]{0,1:T(8,128)} %reduce-scatter.2.cloned.1.call-done), channel_id=1, source_target_pairs={{0,0},{1,8},{2,16},{3,24},{4,32},{5,40},{6,48},{7,56},{8,64},{9,72... | collective-permute-start | bytes 368648 | tf_op jit(solution)/shard_map/ppermute | solution.py:71
  122.4 22.0 %all_gather.10 = f32[192,1280]{0,1:T(8,128)} all-gather(f32[192,160]{0,1:T(8,128)} %reduce-scatter.2.cloned.1.call-done), channel_id=1, replica_groups=mesh['pr'=16,'pc'=8] {'pc'}, dimensions={1}, use_global_device_ids=true | all-gather | bytes 1105920 | tf_op jit(solution)/shard_map/all_gather | solution.py:77
  144.5 0.7 copy-done.8
  145.2 115.9 %all-reduce.2.cloned.1.call-done = f32[192,384]{1,0:T(8,128)} async-done(((f32[192,384]{1,0:T(8,128)}), f32[192,384]{1,0:T(8,128)}) %all-reduce.2.cloned.1.call-update) | async-done | bytes 294928 | tf_op jit(solution)/shard_map/psum | solution.py:80
  261.1 1.2 fusion.105
  262.3 0.2 pad_maximum_fusion.1
  262.5 0.7 slice.178
  263.2 0.7 slice.186
  263.9 0.7 slice.191
  264.6 0.8 slice_dynamic-update-slice_fusion.1
  265.6 0.3 convolution_bitcast_fusion.6
  266.1 0.9 constant_dynamic-update-slice_fusion.8
  267.1 1.4 convolution_subtract_fusion.3
  268.5 0.3 convolution_bitcast_fusion.5
  268.8 0.2 fusion.64
  269.0 0.9 constant_dynamic-update-slice_fusion.7
  269.9 0.8 copy-done.10
  270.8 1.3 convolution_subtract_fusion.5
  272.1 0.3 convolution_bitcast_fusion.4
  272.4 0.2 fusion.62
  272.6 0.9 constant_dynamic-update-slice_fusion.6
  273.7 1.5 convolution_subtract_fusion.4
  275.2 0.3 convolution_bitcast_fusion.3
  275.5 0.2 fusion.60
  276.0 0.9 constant_dynamic-update-slice_fusion.5
  277.0 1.6 convolution_subtract_fusion.2
  278.6 0.3 convolution_bitcast_fusion.2
  279.0 0.9 constant_dynamic-update-slice_fusion.4
  279.9 1.0 slice.200
  280.9 1.7 convolution_subtract_fusion.1
  282.7 0.3 convolution_bitcast_fusion.1
  283.2 0.2 fusion.7
  283.5 0.4 fusion.29
  283.9 0.6 convolution_add_fusion.1
  284.5 0.8 copy.23
  285.4 2.1 fusion.31
  287.5 2.9 fusion.33
  290.4 3.2 convolution_add_fusion
  293.5 14.1 %all-gather.5.cloned.1.call-done = f32[192,2560]{0,1:T(8,128)} async-done(((f32[192,160]{0,1:T(8,128)}), f32[192,2560]{0,1:T(8,128)}) %all-gather.5.cloned.1.call-update) | async-done | bytes 1966096 | tf_op jit(solution)/shard_map/all_gather | solution.py:71
  307.7 23.1 %convolution_subtract_fusion = f32[1280,2560]{1,0:T(8,128)} fusion(f32[1280,2560]{1,0:T(8,128)} %param.3, f32[192,2560]{0,1:T(8,128)} %all-gather.5.cloned.1.call-done, f32[192,2560]{0,1:T(8,128)S(1)} %copy-done, f32[192,1280]{1,0:T(8,128)} %fusion.31, f32[192,1280]{1,0:T(8,128)} %convolution_add_fusion), kind=kOutput, calls=%fused_computation | convolution fusion | flops 7554498560 | bytes 32112640 | tf_op jit(solution)/shard_map/dot_general | solution.py:26
  (60 shorter events, 2.3 us)
Async XLA Ops:
  7.2 64.3 %all-gather.3.cloned.1.call-start = ((), (), s32[]{:S(2)}) async-start(), calls=%async_computation.1 | async-start | bytes 2785280 | tf_op jit(solution)/shard_map/all_gather | solution.py:71
  8.2 9.0 %collective-permute-start = (f32[192,160]{0,1:T(8,128)S(1)}, f32[192,160]{0,1:T(8,128)S(1)}, u32[]{:S(2)}, u32[]{:S(2)}) collective-permute-start(f32[192,160]{0,1:T(8,128)S(1)} %copy.12), channel_id=1, source_target_pairs={{0,0},{1,8},{2,16},{3,24},{4,32},{5,40},{6,48},{7,56},{8,64},{9,72... | collective-permute-start | bytes 368648 | tf_op jit(solution)/shard_map/ppermute | solution.py:71
  17.3 0.7 copy-start.9
  18.0 63.5 %copy-start.2 = (f32[6,32,160]{2,1,0:T(8,128)S(1)}, f32[6,32,160]{2,1,0:T(8,128)}, u32[]{:S(2)}) copy-start(f32[6,32,160]{2,1,0:T(8,128)} %param.4) | copy-start | bytes 368644
  18.0 95.8 %reduce-scatter.2.cloned.1.call-start = ((), (), s32[]{:S(2)}) async-start(), calls=%async_computation.2 | async-start | bytes 1474560 | tf_op jit(solution)/shard_map/reduce_scatter | solution.py:76
  81.5 179.6 %all-reduce.2.cloned.1.call-start = ((), (), s32[]{:S(2)}) async-start(), calls=%async_computation.3 | async-start | bytes 589824 | tf_op jit(solution)/shard_map/psum | solution.py:80
  81.5 4.7 %collective-permute-start.1 = (f32[192,160]{1,0:T(8,128)S(1)}, f32[192,160]{1,0:T(8,128)S(1)}, u32[]{:S(2)}, u32[]{:S(2)}) collective-permute-start(f32[192,160]{1,0:T(8,128)S(1)} %bitcast.71), channel_id=1, source_target_pairs={{0,1},{1,2},{2,3},{3,4},{4,5},{5,6},{6,7},{7,0},{8,9},{9,10},{10,1... | collective-permute-start | bytes 368648 | tf_op jit(solution)/shard_map/ppermute | solution.py:15
  83.6 5.1 %collective-permute-start.2 = (f32[192,160]{1,0:T(8,128)S(1)}, f32[192,160]{1,0:T(8,128)S(1)}, u32[]{:S(2)}, u32[]{:S(2)}) collective-permute-start(f32[192,160]{1,0:T(8,128)S(1)} %bitcast.72), channel_id=1, source_target_pairs={{0,7},{1,0},{2,1},{3,2},{4,3},{5,4},{6,5},{7,6},{8,15},{9,8},{10,9... | collective-permute-start | bytes 368648 | tf_op jit(solution)/shard_map/ppermute | solution.py:18
  86.2 6.0 %collective-permute-start.3 = (f32[192,160]{1,0:T(8,128)S(1)}, f32[192,160]{1,0:T(8,128)S(1)}, u32[]{:S(2)}, u32[]{:S(2)}) collective-permute-start(f32[192,160]{1,0:T(8,128)S(1)} %collective-permute-done.1), channel_id=1, source_target_pairs={{0,1},{1,2},{2,3},{3,4},{4,5},{5,6},{6,7},{7,0},{8,9},{9,10},{10,1... | collective-permute-start | bytes 368648 | tf_op jit(solution)/shard_map/ppermute | solution.py:15
  88.7 7.0 %collective-permute-start.4 = (f32[192,160]{1,0:T(8,128)S(1)}, f32[192,160]{1,0:T(8,128)S(1)}, u32[]{:S(2)}, u32[]{:S(2)}) collective-permute-start(f32[192,160]{1,0:T(8,128)S(1)} %collective-permute-done.2), channel_id=1, source_target_pairs={{0,7},{1,0},{2,1},{3,2},{4,3},{5,4},{6,5},{7,6},{8,15},{9,8},{10,9... | collective-permute-start | bytes 368648 | tf_op jit(solution)/shard_map/ppermute | solution.py:18
  92.2 6.0 %collective-permute-start.5 = (f32[192,160]{1,0:T(8,128)S(1)}, f32[192,160]{1,0:T(8,128)S(1)}, u32[]{:S(2)}, u32[]{:S(2)}) collective-permute-start(f32[192,160]{1,0:T(8,128)S(1)} %collective-permute-done.3), channel_id=1, source_target_pairs={{0,1},{1,2},{2,3},{3,4},{4,5},{5,6},{6,7},{7,0},{8,9},{9,10},{10,1... | collective-permute-start | bytes 368648 | tf_op jit(solution)/shard_map/ppermute | solution.py:15
  95.7 14.7 %collective-permute-start.6 = (f32[192,160]{1,0:T(8,128)S(1)}, f32[192,160]{1,0:T(8,128)S(1)}, u32[]{:S(2)}, u32[]{:S(2)}) collective-permute-start(f32[192,160]{1,0:T(8,128)S(1)} %collective-permute-done.4), channel_id=1, source_target_pairs={{0,7},{1,0},{2,1},{3,2},{4,3},{5,4},{6,5},{7,6},{8,15},{9,8},{10,9... | collective-permute-start | bytes 368648 | tf_op jit(solution)/shard_map/ppermute | solution.py:18
  98.2 13.8 %collective-permute-start.7 = (f32[192,160]{1,0:T(8,128)S(1)}, f32[192,160]{1,0:T(8,128)S(1)}, u32[]{:S(2)}, u32[]{:S(2)}) collective-permute-start(f32[192,160]{1,0:T(8,128)S(1)} %collective-permute-done.5), channel_id=1, source_target_pairs={{0,1},{1,2},{2,3},{3,4},{4,5},{5,6},{6,7},{7,0},{8,9},{9,10},{10,1... | collective-permute-start | bytes 368648 | tf_op jit(solution)/shard_map/ppermute | solution.py:15
  113.8 171.6 %copy-start.1 = (f32[192,1280]{1,0:T(8,128)}, f32[192,1280]{1,0:T(8,128)S(1)}, u32[]{:S(2)}) copy-start(f32[192,1280]{1,0:T(8,128)S(1)} %dynamic_update_slice.31) | copy-start | bytes 2949124
  116.2 191.4 %all-gather.5.cloned.1.call-start = ((), (), s32[]{:S(2)}) async-start(), calls=%async_computation.4 | async-start | bytes 2785280 | tf_op jit(solution)/shard_map/all_gather | solution.py:71
  116.3 28.2 %collective-permute-start.8 = (f32[192,160]{0,1:T(8,128)}, f32[192,160]{0,1:T(8,128)S(1)}, u32[]{:S(2)}, u32[]{:S(2)}) collective-permute-start(f32[192,160]{0,1:T(8,128)} %reduce-scatter.2.cloned.1.call-done), channel_id=1, source_target_pairs={{0,0},{1,8},{2,16},{3,24},{4,32},{5,40},{6,48},{7,56},{8,64},{9,72... | collective-permute-start | bytes 368648 | tf_op jit(solution)/shard_map/ppermute | solution.py:71
  144.5 0.7 copy-start.8
  145.2 120.5 %copy-start.7 = (f32[6,32,32]{2,1,0:T(8,128)S(1)}, f32[6,32,32]{2,1,0:T(8,128)}, u32[]{:S(2)}) copy-start(f32[6,32,32]{2,1,0:T(8,128)} %param.5) | copy-start | bytes 73732
  261.1 4.3 %copy-start.6 = (f32[192,384]{1,0:T(8,128)S(1)}, f32[192,384]{1,0:T(8,128)}, u32[]{:S(2)}) copy-start(f32[192,384]{1,0:T(8,128)} %all-reduce.2.cloned.1.call-done) | copy-start | bytes 884740
  262.5 3.4 %copy-start.4 = (f32[192,576]{1,0:T(8,128)}, f32[192,576]{1,0:T(8,128)S(1)}, u32[]{:S(2)}) copy-start(f32[192,576]{1,0:T(8,128)S(1)} %get-tuple-element.5) | copy-start | bytes 1327108
  267.0 2.0 copy-start.3
  269.9 0.8 copy-start.10
  275.7 7.8 %copy-start.5 = (f32[192,160]{0,1:T(8,128)S(1)}, f32[192,160]{0,1:T(8,128)}, u32[]{:S(2)}) copy-start(f32[192,160]{0,1:T(8,128)} %reduce-scatter.2.cloned.1.call-done) | copy-start | bytes 368644
  287.5 20.2 %copy-start = (f32[192,2560]{0,1:T(8,128)S(1)}, f32[192,2560]{0,1:T(8,128)}, u32[]{:S(2)}) copy-start(f32[192,2560]{0,1:T(8,128)} %all-gather.3.cloned.1.call-done) | copy-start | bytes 5898244
Sparse Core Ops, SparseCore 0:
  18.1 53.3 all-gather.2
  81.6 30.1 reduce-scatter.1
  117.1 143.9 all-reduce.1
  263.1 44.5 all-gather.4
